TPU v7x, 256 devices: a whole 4x4x8 slice. The times are simulated.
256 devices in a mesh: pop: 32 (over z_hi, x, core), shard: 8 (over z_lo, y).
Axes of the slice: x: 4, y: 4, z: 8 (z_hi: 4, z_lo: 2; z = z_hi * 2 + z_lo), core: 2. Of those that a mesh axis runs over, the one named last changes fastest.
Arguments:
- hidden: bfloat16 [64, 4096, 4096], P('pop', 'shard'), may hold values from -6 to 6
- norm_scale_vector: float32 [4096], replicated, may hold values from 0.3 to 3
- w_value: bfloat16 [4096, 1024], P('shard'), may hold values from -0.09375 to 0.09375
- model_side_factor: bfloat16 [64, 4, 4096], P('pop'), may hold values from -0.09375 to 0.09375
- value_side_factor: bfloat16 [64, 4, 1024], P('pop'), may hold values from -3 to 3
- target: bfloat16 [64, 4096, 1024], P('pop', 'shard'), may hold values from -6 to 6
- lengths: int32 [64], P('pop'), may hold values from 1 to 4096, 163840 in all
- fitness_ranks: int32 [64], replicated, may hold values from 0 to 63, each once
Outputs:
- losses: float32 [64, 4096], P('pop', 'shard')
- scores: float32 [64], P('pop')
- weight_step: bfloat16 [4096, 1024], P('shard')
Inputs may be any that keep to these rules, and one draw needn't show every extreme that they name: Positions t < lengths[m] of member m are live; the lengths of all members sum to 163840, and some member has exactly 4096. `fitness_ranks`: each of 0 to 63 appears once.
All inputs are finite; a program needn't handle non-finite values. No bound on the sum of `lengths` on one device may be relied on, other than what follows from the above.
Results may differ from a plain program's by a relative error of at most 0.0048.
Values may be sent and summed in bfloat16 or wider, within the bound.
A program may use at most 64 MiB of HBM per device.

v0:
```python
import math
import jax
import jax.numpy as jnp
from jax import lax
from jax.sharding import PartitionSpec as P

noise_scale = 0.1
epsilon = 1e-05


def on_device(
    hidden,
    norm_scale_vector,
    w_value,
    model_side_factor,
    value_side_factor,
    target,
    lengths,
    fitness_ranks,
):
    members, span_here, width = hidden.shape
    share, outputs = w_value.shape
    everyone = fitness_ranks.shape[0]
    widened = hidden.astype(jnp.float32)
    inverse = lax.rsqrt(jnp.mean(widened * widened, axis=-1, keepdims=True) + epsilon)
    normalized_input = (widened * inverse * norm_scale_vector).astype(jnp.bfloat16)
    flattened = normalized_input.reshape(members * span_here, width)
    projected = jnp.dot(
        flattened,
        lax.all_gather(w_value, "shard", axis=0, tiled=True),
        preferred_element_type=jnp.float32,
    )
    reduced_output = jnp.einsum(
        "uch,ufh->ucf", normalized_input, model_side_factor, preferred_element_type=jnp.float32
    ).astype(jnp.bfloat16)
    lateral_product = jnp.einsum(
        "nfw,nwx->nfx", reduced_output, value_side_factor, preferred_element_type=jnp.float32
    )
    values = projected.reshape(members, span_here, outputs) + noise_scale * lateral_product
    errors = values - target.astype(jnp.float32)
    squared = jnp.mean(errors * errors, axis=-1)
    first_position = lax.axis_index("shard") * span_here
    position = first_position + lax.broadcasted_iota(jnp.int32, (members, span_here), 1)
    losses = jnp.where(position < lengths[:, None], squared, 0.0)
    totals = lax.psum(jnp.sum(losses, axis=1), "shard")
    scores = totals / lengths.astype(jnp.float32)
    column_start = lax.axis_index("shard") * share
    left_rows = lax.dynamic_slice_in_dim(model_side_factor, column_start, share, 2)
    step_factor = math.sqrt(width) / (noise_scale * everyone)
    own_ranks = lax.dynamic_slice_in_dim(fitness_ranks, lax.axis_index("pop") * members, members, 0)
    own_fitness = own_ranks.astype(jnp.float32) / (everyone - 1) - 0.5
    scaled_left = (left_rows.astype(jnp.float32) * own_fitness[:, None, None]).astype(jnp.bfloat16)
    pack = jnp.concatenate([scaled_left, value_side_factor], axis=2)
    pack = pack.reshape(pack.shape[0] * pack.shape[1], pack.shape[2])
    everything = lax.all_gather(pack, "pop", axis=0, tiled=True)
    summed_step = lax.dot_general(
        everything[:, :share],
        everything[:, share:],
        (((0,), (0,)), ((), ())),
        preferred_element_type=jnp.float32,
    )
    weight_step = (summed_step * step_factor).astype(jnp.bfloat16)
    return (losses, scores, weight_step)


def solution(mesh):
    placed = (
        P("pop", "shard", None),
        P(),
        P("shard", None),
        P("pop", None, None),
        P("pop", None, None),
        P("pop", "shard", None),
        P("pop"),
        P(),
    )
    return jax.shard_map(
        on_device,
        mesh=mesh,
        in_specs=placed,
        out_specs=(P("pop", "shard"), P("pop"), P("shard", None)),
        check_vma=False,
    )
```

profile of v0, /device:TPU:6, one launch (start us, length us, event | category | flops | bytes accessed | tf_op | source)
XLA Modules:
  0.0 162.0 jit_solution(4412377680226571423)
XLA Ops:
  7.2 0.0 copy-start.4
  7.2 0.0 all-gather.2.cloned.1.call-start
  7.2 0.7 all-gather.2.cloned.1.call-update
  7.9 0.7 multiply_add_fusion
  8.7 0.8 multiply_convert_fusion.1
  9.4 0.7 pad_maximum_fusion
  10.2 5.1 %fusion = f32[2,512]{1,0:T(2,128)S(1)} fusion(bf16[2,512,4096]{2,1,0:T(8,128)(2,1)} %param.8), kind=kLoop, calls=%fused_computation.2 | loop fusion | flops 12581888 | bytes 8392704 | tf_op jit(solution)/shard_map/reduce_sum | solution.py:25
  15.3 41.3 %all_gather.7 = bf16[256,1536]{1,0:T(8,128)(2,1)S(1)} all-gather(bf16[8,1536]{1,0:T(8,128)(2,1)S(1)} %reshape.24), channel_id=1, replica_groups=mesh['pop'=32,'shard'=8] {'pop'}, dimensions={0}, use_global_device_ids=true | all-gather | bytes 811008 | tf_op jit(solution)/shard_map/all_gather | solution.py:55
  56.6 1.4 multiply_convert_fusion
  58.0 0.0 copy-start
  58.0 0.0 copy-start.1
  58.0 0.0 copy-start.3
  58.0 51.7 %all-gather.2.cloned.1.call-done = bf16[4096,1024]{1,0:T(8,128)(2,1)} async-done(((bf16[512,1024]{1,0:T(8,128)(2,1)}), bf16[4096,1024]{1,0:T(8,128)(2,1)}) %all-gather.2.cloned.1.call-update) | async-done | bytes 8388624 | tf_op jit(solution)/shard_map/all_gather | solution.py:30
  109.7 0.0 copy-done.4
  109.7 15.1 %fusion.3 = f32[2,512,1024]{2,1,0:T(8,128)} fusion(bf16[4096,1024]{1,0:T(8,128)(2,1)} %all-gather.2.cloned.1.call-done, bf16[2,512,4096]{2,1,0:T(8,128)(2,1)} %param.8, f32[4096]{0:T(1024)S(1)} %copy-done.4, f32[2,512]{1,0:T(2,128)S(1)} %add_rsqrt_fusion), kind=kOutput, calls=%fused_computation.5 | convolution fusion | flops 8606711808 | bytes 20992000 | tf_op jit(solution)/shard_map/dot_general | solution.py:28
  124.8 0.0 copy-done
  124.8 0.0 copy-done.1
  124.8 0.0 copy-done.3
  124.8 0.0 copy-start.2
  124.8 8.0 %multiply_reduce_fusion = f32[2,512]{1,0:T(2,128)S(1)} fusion(bf16[2,512,1024]{2,1,0:T(8,128)(2,1)S(1)} %copy-done.3, f32[2,512,1024]{2,1,0:T(8,128)} %fusion.3, bf16[2,4,1024]{2,1,0:T(4,128)(2,1)S(1)} %copy-done, bf16[2,4,4096]{2,1,0:T(4,128)(2,1)S(1)} %copy-done.1, bf16[2,512,4096]{2,1,0:T(8,128)(2,1)} %param.8, f32[4096]{0:T(1024)S(1)} %copy-done.4, ...), kind=kOutput, calls=%fused_computation.8 | convolution fusion | flops 65014784 | bytes 14786560 | tf_op jit(solution)/shard_map/nfw,nwx->nfx/dot_general | solution.py:36
  132.9 0.0 copy-done.2
  132.9 0.8 fusion.15
  133.6 21.0 %psum.7 = f32[2]{0:T(128)S(1)} all-reduce(f32[2]{0:T(128)S(1)} %get-tuple-element.3), channel_id=1, replica_groups=mesh['pop'=32,'shard'=8] {'shard'}, use_global_device_ids=true, to_apply=%region_3.4 | all-reduce | flops 2 | bytes 16 | tf_op jit(solution)/shard_map/psum | solution.py:45
  154.6 0.5 convert_divide_fusion
  (3 shorter events, 0.0 us)
Async XLA Ops:
  7.2 102.6 %copy-start.4 = (f32[4096]{0:T(1024)S(1)}, f32[4096]{0:T(1024)}, u32[]{:S(2)}) copy-start(f32[4096]{0:T(1024)} %param.9) | copy-start | bytes 49156
  7.2 102.6 %all-gather.2.cloned.1.call-start = ((), (), s32[]{:S(2)}) async-start(), calls=%async_computation | async-start | bytes 9437184 | tf_op jit(solution)/shard_map/all_gather | solution.py:30
  58.0 66.8 %copy-start = (bf16[2,4,1024]{2,1,0:T(4,128)(2,1)S(1)}, bf16[2,4,1024]{2,1,0:T(4,128)(2,1)}, u32[]{:S(2)}) copy-start(bf16[2,4,1024]{2,1,0:T(4,128)(2,1)} %param.12) | copy-start | bytes 49156
  58.0 66.8 %copy-start.1 = (bf16[2,4,4096]{2,1,0:T(4,128)(2,1)S(1)}, bf16[2,4,4096]{2,1,0:T(4,128)(2,1)}, u32[]{:S(2)}) copy-start(bf16[2,4,4096]{2,1,0:T(4,128)(2,1)} %param.11) | copy-start | bytes 196612
  58.0 66.8 %copy-start.3 = (bf16[2,512,1024]{2,1,0:T(8,128)(2,1)S(1)}, bf16[2,512,1024]{2,1,0:T(8,128)(2,1)}, u32[]{:S(2)}) copy-start(bf16[2,512,1024]{2,1,0:T(8,128)(2,1)} %param.13) | copy-start | bytes 6291460
  124.8 8.0 %copy-start.2 = (s32[2]{0:T(128)S(1)}, s32[2]{0:T(128)}, u32[]{:S(2)}) copy-start(s32[2]{0:T(128)} %param.14) | copy-start | bytes 28
Sparse Core Ops, SparseCore 0:
  9.8 99.8 all-gather.1
where the time goes:
time: 162 us
  blocking collectives  62.3 us (38%)
  waiting for transfers between devices  52.4 us (32%)
  matrix products  24.5 us (15%)
  between operations  14.1 us (9%)
  other arithmetic  8.63 us (5%)
    all_gather x1, waiting for transfers between devices, on_device(): lax.all_gather(w_value, 'shard', axis=0, tiled=True)  51.7 us
    all_gather x1, blocking collectives, on_device(): everything = lax.all_gather(pack, 'pop', axis=0, tiled=True)  41.3 us
    psum x1, blocking collectives, on_device(): totals = lax.psum(jnp.sum(losses, axis=1), 'shard')  21 us
    dot_general x1, matrix products, on_device(): jnp.dot(flattened, lax.all_gather(w_value, 'shard', axis=0, tiled=True),...  15.1 us
    dot_general x1, matrix products, on_device(): jnp.einsum('nfw,nwx->nfx', reduced_output, value_side_factor, preferred_e...  8 us
    reduce_sum x1, other arithmetic, on_device(): jnp.mean(widened * widened, axis=-1, keepdims=True) + epsilon  5.08 us
  transfers between devices with their start and end apart: 1, of which 1 were waited for; matrix products, arithmetic and copies ran while one was open for 5% of the time, Pallas kernels for 0%

commit v1 on v0

--- a/solution.py
+++ b/solution.py
@@ -52,7 +52,16 @@
     scaled_left = (left_rows.astype(jnp.float32) * own_fitness[:, None, None]).astype(jnp.bfloat16)
     pack = jnp.concatenate([scaled_left, value_side_factor], axis=2)
     pack = pack.reshape(pack.shape[0] * pack.shape[1], pack.shape[2])
-    everything = lax.all_gather(pack, "pop", axis=0, tiled=True)
+    obtain_weights = lambda patch, net_axis: jnp.concatenate(
+        jax.lax.all_to_all(
+            jnp.stack([patch for _ in range(jax.lax.axis_size(net_axis))]),
+            net_axis,
+            concat_axis=0,
+            split_axis=0,
+        ),
+        axis=0,
+    )
+    everything = obtain_weights(pack, "pop")
     summed_step = lax.dot_general(
         everything[:, :share],
         everything[:, share:],

time: 162 us -> 172 us (1.062)
  blocking collectives: 62.3 us -> 16.6 us
  waiting for transfers between devices: 52.4 us -> 94.5 us
  starting transfers between devices: 0.04 us -> 11.6 us
    all_gather x1 -> x0, blocking collectives: 41.3 us -> none  [on_device(): everything = lax.all_gather(pack, 'pop', axis=0, tiled=True)]
    all_to_all x0 -> x1, waiting for transfers between devices: none -> 25.7 us  [on_device(): jax.lax.all_to_all(jnp.stack([patch for _ in range(jax.lax.axis_size(net_...]
    all_gather x1, waiting for transfers between devices: 51.7 us -> 68.1 us  [on_device(): lax.all_gather(w_value, 'shard', axis=0, tiled=True)]
    all_to_all x0 -> x1, starting transfers between devices: none -> 11.6 us  [on_device(): jax.lax.all_to_all(jnp.stack([patch for _ in range(jax.lax.axis_size(net_...]
    psum x1, blocking collectives: 21 us -> 16.6 us  [on_device(): totals = lax.psum(jnp.sum(losses, axis=1), 'shard')]
  transfers between devices with their start and end apart: 1 -> 2, of which waited for: 1 -> 2; matrix products, arithmetic and copies ran while one was open for 5% -> 6% of each run, Pallas kernels for 0% -> 0%
where the time goes in v1:
time: 172 us; the launch traced here: 171 us
  waiting for transfers between devices  94.5 us (55%)
  matrix products  24.5 us (14%)
  blocking collectives  16.6 us (10%)
  between operations  14.1 us (8%)
  starting transfers between devices  11.6 us (7%)
  other arithmetic  8.98 us (5%)
    all_gather x1, waiting for transfers between devices, on_device(): lax.all_gather(w_value, 'shard', axis=0, tiled=True)  68.1 us
    all_to_all x1, waiting for transfers between devices, on_device(): jax.lax.all_to_all(jnp.stack([patch for _ in range(jax.lax.axis_size(net_...  25.7 us
    psum x1, blocking collectives, on_device(): totals = lax.psum(jnp.sum(losses, axis=1), 'shard')  16.6 us
    dot_general x1, matrix products, on_device(): jnp.dot(flattened, lax.all_gather(w_value, 'shard', axis=0, tiled=True),...  15.1 us
    all_to_all x1, starting transfers between devices, on_device(): jax.lax.all_to_all(jnp.stack([patch for _ in range(jax.lax.axis_size(net_...  11.6 us
    dot_general x1, matrix products, on_device(): jnp.einsum('nfw,nwx->nfx', reduced_output, value_side_factor, preferred_e...  7.98 us
    reduce_sum x1, other arithmetic, on_device(): jnp.mean(widened * widened, axis=-1, keepdims=True) + epsilon  5.43 us
  transfers between devices with their start and end apart: 2, of which 2 were waited for; matrix products, arithmetic and copies ran while one was open for 6% of the time, Pallas kernels for 0%

profile of v1, /device:TPU:6, one launch (start us, length us, event | category | flops | bytes accessed | tf_op | source)
XLA Modules:
  0.0 171.2 jit_solution(2653734034494230441)
XLA Ops:
  7.2 0.0 copy-start.4
  7.2 0.0 all-gather.2.cloned.1.call-start
  7.2 0.7 all-gather.2.cloned.1.call-update
  7.9 0.7 multiply_add_fusion
  8.7 0.8 multiply_convert_fusion.1
  9.4 0.7 pad_maximum_fusion
  10.2 0.9 stack.3
  11.1 11.6 %all-to-all-start = ((bf16[32,8,1536]{2,1,0:T(8,128)(2,1)}), bf16[32,8,1536]{2,1,0:T(8,128)(2,1)S(1)}, u32[]{:S(2)}, u32[]{:S(2)}) async-start(bf16[32,8,1536]{2,1,0:T(8,128)(2,1)} %stack.3), calls=%async_computation | async-start | bytes 1572864 | tf_op jit(solution)/shard_map/all_to_all | solution.py:56
  22.7 5.4 %fusion = f32[2,512]{1,0:T(2,128)S(1)} fusion(bf16[2,512,4096]{2,1,0:T(8,128)(2,1)} %param.8), kind=kLoop, calls=%fused_computation.2 | loop fusion | flops 12581888 | bytes 8392704 | tf_op jit(solution)/shard_map/reduce_sum | solution.py:25
  28.1 25.7 %all-to-all-done = bf16[32,8,1536]{2,1,0:T(8,128)(2,1)S(1)} async-done(((bf16[32,8,1536]{2,1,0:T(8,128)(2,1)}), bf16[32,8,1536]{2,1,0:T(8,128)(2,1)S(1)}, u32[]{:S(2)}, u32[]{:S(2)}) %all-to-all-start) | async-done | bytes 786464 | tf_op jit(solution)/shard_map/all_to_all | solution.py:56
  53.8 1.4 multiply_convert_fusion
  55.3 0.0 copy-start
  55.3 0.0 copy-start.1
  55.3 0.0 copy-start.3
  55.3 68.1 %all-gather.2.cloned.1.call-done = bf16[4096,1024]{1,0:T(8,128)(2,1)} async-done(((bf16[512,1024]{1,0:T(8,128)(2,1)}), bf16[4096,1024]{1,0:T(8,128)(2,1)}) %all-gather.2.cloned.1.call-update) | async-done | bytes 8388624 | tf_op jit(solution)/shard_map/all_gather | solution.py:30
  123.4 0.0 copy-done.4
  123.4 15.1 %fusion.3 = f32[2,512,1024]{2,1,0:T(8,128)} fusion(bf16[4096,1024]{1,0:T(8,128)(2,1)} %all-gather.2.cloned.1.call-done, bf16[2,512,4096]{2,1,0:T(8,128)(2,1)} %param.8, f32[4096]{0:T(1024)S(1)} %copy-done.4, f32[2,512]{1,0:T(2,128)S(1)} %add_rsqrt_fusion), kind=kOutput, calls=%fused_computation.5 | convolution fusion | flops 8606711808 | bytes 20992000 | tf_op jit(solution)/shard_map/dot_general | solution.py:28
  138.5 0.0 copy-done
  138.5 0.0 copy-done.1
  138.5 0.0 copy-done.3
  138.5 0.0 copy-start.2
  138.5 8.0 %multiply_reduce_fusion = f32[2,512]{1,0:T(2,128)S(1)} fusion(bf16[2,512,1024]{2,1,0:T(8,128)(2,1)S(1)} %copy-done.3, f32[2,512,1024]{2,1,0:T(8,128)} %fusion.3, bf16[2,4,1024]{2,1,0:T(4,128)(2,1)S(1)} %copy-done, bf16[2,4,4096]{2,1,0:T(4,128)(2,1)S(1)} %copy-done.1, bf16[2,512,4096]{2,1,0:T(8,128)(2,1)} %param.8, f32[4096]{0:T(1024)S(1)} %copy-done.4, ...), kind=kOutput, calls=%fused_computation.8 | convolution fusion | flops 65014784 | bytes 14786560 | tf_op jit(solution)/shard_map/nfw,nwx->nfx/dot_general | solution.py:36
  146.5 0.0 copy-done.2
  146.5 0.8 fusion.15
  147.2 16.6 %psum.7 = f32[2]{0:T(128)S(1)} all-reduce(f32[2]{0:T(128)S(1)} %get-tuple-element.3), channel_id=1, replica_groups=mesh['pop'=32,'shard'=8] {'shard'}, use_global_device_ids=true, to_apply=%region_3.4 | all-reduce | flops 2 | bytes 16 | tf_op jit(solution)/shard_map/psum | solution.py:45
  163.8 0.5 convert_divide_fusion
  (3 shorter events, 0.0 us)
Async XLA Ops:
  7.2 116.2 %copy-start.4 = (f32[4096]{0:T(1024)S(1)}, f32[4096]{0:T(1024)}, u32[]{:S(2)}) copy-start(f32[4096]{0:T(1024)} %param.9) | copy-start | bytes 49156
  7.2 116.2 %all-gather.2.cloned.1.call-start = ((), (), s32[]{:S(2)}) async-start(), calls=%async_computation.1 | async-start | bytes 9437184 | tf_op jit(solution)/shard_map/all_gather | solution.py:30
  11.1 42.7 %all-to-all-start = ((bf16[32,8,1536]{2,1,0:T(8,128)(2,1)}), bf16[32,8,1536]{2,1,0:T(8,128)(2,1)S(1)}, u32[]{:S(2)}, u32[]{:S(2)}) async-start(bf16[32,8,1536]{2,1,0:T(8,128)(2,1)} %stack.3), calls=%async_computation | async-start | bytes 1572864 | tf_op jit(solution)/shard_map/all_to_all | solution.py:56
  55.3 83.2 %copy-start = (bf16[2,4,1024]{2,1,0:T(4,128)(2,1)S(1)}, bf16[2,4,1024]{2,1,0:T(4,128)(2,1)}, u32[]{:S(2)}) copy-start(bf16[2,4,1024]{2,1,0:T(4,128)(2,1)} %param.12) | copy-start | bytes 49156
  55.3 83.2 %copy-start.1 = (bf16[2,4,4096]{2,1,0:T(4,128)(2,1)S(1)}, bf16[2,4,4096]{2,1,0:T(4,128)(2,1)}, u32[]{:S(2)}) copy-start(bf16[2,4,4096]{2,1,0:T(4,128)(2,1)} %param.11) | copy-start | bytes 196612
  55.3 83.2 %copy-start.3 = (bf16[2,512,1024]{2,1,0:T(8,128)(2,1)S(1)}, bf16[2,512,1024]{2,1,0:T(8,128)(2,1)}, u32[]{:S(2)}) copy-start(bf16[2,512,1024]{2,1,0:T(8,128)(2,1)} %param.13) | copy-start | bytes 6291460
  138.5 8.0 %copy-start.2 = (s32[2]{0:T(128)S(1)}, s32[2]{0:T(128)}, u32[]{:S(2)}) copy-start(s32[2]{0:T(128)} %param.14) | copy-start | bytes 28
Sparse Core Ops, SparseCore 0:
  9.8 113.5 all-gather.1
